TPU v7x, 512 devices: a whole 4x8x8 slice. The times are simulated.
512 devices in a mesh: rows: 16 (over x_lo, z), cols: 32 (over y, x_hi, core).
Axes of the slice: x: 4 (x_hi: 2, x_lo: 2; x = x_hi * 2 + x_lo), y: 8, z: 8, core: 2. Of those that a mesh axis runs over, the one named last changes fastest.
Arguments:
- tokens: bfloat16 [128, 1024, 192], P('rows', 'cols'), may hold values from -60 to 60
- region_ids: int32 [128, 1024], P('rows', 'cols'), may hold values from 0 to 2
- upper_rim: bfloat16 [4, 1024, 192], P(None, 'cols'), may hold values from -60 to 60
- upper_ids: int32 [4, 1024], P(None, 'cols'), may hold values from 0 to 2
- lower_rim: bfloat16 [4, 1024, 192], P(None, 'cols'), may hold values from -60 to 60
- lower_ids: int32 [4, 1024], P(None, 'cols'), may hold values from 0 to 2
- cotangent: bfloat16 [128, 1024, 192], P('rows', 'cols'), may hold values from -6 to 6
- qkv_weight: bfloat16 [2, 192, 576], replicated, may hold values from -0.4375 to 0.4375
- proj_weight: bfloat16 [2, 192, 192], replicated, may hold values from -0.4375 to 0.4375
- inner_weight: bfloat16 [2, 192, 768], replicated, may hold values from -0.4375 to 0.4375
- outer_weight: bfloat16 [2, 768, 192], replicated, may hold values from -0.21875 to 0.21875
- bias_table: float32 [2, 225, 6], replicated, may hold values from -4 to 400
Outputs:
- token_grad: bfloat16 [128, 1024, 192], P('rows', 'cols')
- qkv_grad: float32 [2, 192, 576], P(None, 'rows', 'cols')
- proj_grad: float32 [2, 192, 192], P(None, 'rows', 'cols')
- inner_grad: float32 [2, 192, 768], P(None, 'rows', 'cols')
- outer_grad: float32 [2, 768, 192], P(None, 'rows', 'cols')
- table_grad: float32 [2, 225, 6], replicated
All inputs are finite; a program needn't handle non-finite values.
Results may differ from a plain program's by a relative error of at most 0.03.
Values may be sent and summed in bfloat16 or wider, within the bound.
A program may use at most 64 MiB of HBM per device.

v0:
```python
import jax
import jax.numpy as jnp
from jax import lax
from jax.sharding import PartitionSpec as P

WIN = 8
HALF = 4
BIAS_LEN = 225
EPS = 1e-05
MASKED = -1000000000.0


def with_halo(block, sides, width, periodic):
    for axis, dim in sides:
        count = lax.axis_size(axis)
        forward = [(i, i + 1) for i in range(count - 1)]
        if periodic:
            forward.append((count - 1, 0))
        backward = [(target, source) for source, target in forward]
        low = lax.ppermute(
            lax.slice_in_dim(block, block.shape[dim] - width, None, axis=dim), axis, forward
        )
        high = lax.ppermute(lax.slice_in_dim(block, 0, width, axis=dim), axis, backward)
        block = jnp.concatenate([low, block, high], axis=dim)
    return block


def normalize(values):
    center = jnp.mean(values, axis=-1, keepdims=True)
    shifted = values - center
    spread = jnp.mean(shifted * shifted, axis=-1, keepdims=True)
    return shifted * lax.rsqrt(spread + EPS)


def norm_back(source, grad_norm):
    _, pullback = jax.vjp(normalize, source.astype(jnp.float32))
    return pullback(grad_norm)[0]


def by_transpose(left, right):
    return lax.dot_general(
        left, right, (((1,), (1,)), ((), ())), preferred_element_type=jnp.float32
    )


def over_rows(left, right):
    return lax.dot_general(
        left, right, (((0,), (0,)), ((), ())), preferred_element_type=jnp.float32
    )


def windows(surface):
    grid_rows, grid_cols = (surface.shape[0], surface.shape[1])
    trailing = surface.shape[2:]
    blocked = surface.reshape((grid_rows // WIN, WIN, grid_cols // WIN, WIN) + trailing)
    permute = (0, 2, 1, 3) + tuple(range(4, 4 + len(trailing)))
    return blocked.transpose(permute).reshape(
        (grid_rows // WIN * (grid_cols // WIN), WIN * WIN) + trailing
    )


def unwindows(framed, grid_rows, grid_cols):
    trailing = framed.shape[2:]
    blocked = framed.reshape((grid_rows // WIN, grid_cols // WIN, WIN, WIN) + trailing)
    permute = (0, 2, 1, 3) + tuple(range(4, 4 + len(trailing)))
    return blocked.transpose(permute).reshape((grid_rows, grid_cols) + trailing)


def relative_onehot():
    places = jnp.arange(WIN * WIN, dtype=jnp.int32)
    pos_row = places // WIN
    pos_col = places % WIN
    lookup = (
        (pos_row[:, None] - pos_row[None, :] + WIN - 1) * (2 * WIN - 1)
        + pos_col[:, None]
        - pos_col[None, :]
        + WIN
        - 1
    )
    return (lookup[:, :, None] == jnp.arange(BIAS_LEN, dtype=jnp.int32)[None, None, :]).astype(
        jnp.float32
    )


def attend(normed_win, ids_win, qkv_weight, pos_bias):
    window_count, window_size, channels = normed_win.shape
    head_count = pos_bias.shape[0]
    head_size = channels // head_count
    score_scale = head_size ** (-0.5)
    qkv_all = jnp.dot(
        normed_win.reshape(window_count * window_size, channels),
        qkv_weight,
        preferred_element_type=jnp.float32,
    )
    qkv_all = qkv_all.astype(jnp.bfloat16).reshape(
        window_count, window_size, 3, head_count, head_size
    )
    scores = jnp.einsum(
        "nqhd,nkhd->nhqk", qkv_all[:, :, 0], qkv_all[:, :, 1], preferred_element_type=jnp.float32
    )
    scores = scores * score_scale + pos_bias[None]
    same_region = ids_win[:, :, None] == ids_win[:, None, :]
    scores = jnp.where(same_region[:, None], scores, MASKED)
    row_max = jnp.max(scores, axis=-1, keepdims=True)
    exponent = jnp.exp(scores - row_max)
    attn_probs = exponent / jnp.sum(exponent, axis=-1, keepdims=True)
    attn_out = jnp.einsum(
        "nhqk,nkhd->nqhd",
        attn_probs.astype(jnp.bfloat16),
        qkv_all[:, :, 2],
        preferred_element_type=jnp.float32,
    )
    return (
        qkv_all,
        attn_probs,
        attn_out.astype(jnp.bfloat16).reshape(window_count, window_size, channels),
    )


def attend_back(normed_win, qkv_all, attn_probs, grad_out, qkv_weight):
    window_count, window_size, channels = normed_win.shape
    head_count, head_size = (qkv_all.shape[3], qkv_all.shape[4])
    score_scale = head_size ** (-0.5)
    grad_heads = grad_out.reshape(window_count, window_size, head_count, head_size)
    grad_probs = jnp.einsum(
        "nqhd,nkhd->nhqk", grad_heads, qkv_all[:, :, 2], preferred_element_type=jnp.float32
    )
    grad_scores = attn_probs * (
        grad_probs - jnp.sum(grad_probs * attn_probs, axis=-1, keepdims=True)
    )
    grad_bias = jnp.sum(grad_scores, axis=0)
    scores_low = grad_scores.astype(jnp.bfloat16)
    grad_query = (
        jnp.einsum(
            "nhqk,nkhd->nqhd", scores_low, qkv_all[:, :, 1], preferred_element_type=jnp.float32
        )
        * score_scale
    )
    grad_key = (
        jnp.einsum(
            "nhqk,nqhd->nkhd", scores_low, qkv_all[:, :, 0], preferred_element_type=jnp.float32
        )
        * score_scale
    )
    grad_value = jnp.einsum(
        "nhqk,nqhd->nkhd",
        attn_probs.astype(jnp.bfloat16),
        grad_heads,
        preferred_element_type=jnp.float32,
    )
    grad_qkv = jnp.stack([grad_query, grad_key, grad_value], axis=2).astype(jnp.bfloat16)
    grad_qkv = grad_qkv.reshape(window_count * window_size, 3 * channels)
    flattened = normed_win.reshape(window_count * window_size, channels)
    grad_norm = by_transpose(grad_qkv, qkv_weight)
    grad_weight = over_rows(flattened, grad_qkv)
    return (grad_norm.reshape(window_count, window_size, channels), grad_weight, grad_bias)


def mixer_forward(surface, region, qkv_weight, table):
    grid_rows, grid_cols = (surface.shape[0], surface.shape[1])
    normed = normalize(surface.astype(jnp.float32)).astype(jnp.bfloat16)
    pos_bias = jnp.einsum("ijb,bh->hij", relative_onehot(), table, precision=lax.Precision.HIGHEST)
    qkv_all, attn_probs, attn_out = attend(windows(normed), windows(region), qkv_weight, pos_bias)
    return (normed, qkv_all, attn_probs, unwindows(attn_out, grid_rows, grid_cols))


def mixer_backward(surface, normed, qkv_all, attn_probs, grad_mix, qkv_weight):
    grid_rows, grid_cols = (surface.shape[0], surface.shape[1])
    grad_norm, grad_weight, grad_bias = attend_back(
        windows(normed), qkv_all, attn_probs, windows(grad_mix), qkv_weight
    )
    grad_surface = norm_back(surface, unwindows(grad_norm, grid_rows, grid_cols))
    grad_table = jnp.einsum(
        "ijb,hij->bh", relative_onehot(), grad_bias, precision=lax.Precision.HIGHEST
    )
    return (grad_surface, grad_weight, grad_table)


def channel_forward(middle, inner_w, outer_w):
    normed = normalize(middle.astype(jnp.float32)).astype(jnp.bfloat16)
    hidden_pre = jnp.dot(normed, inner_w, preferred_element_type=jnp.float32)
    hidden_act = jax.nn.gelu(hidden_pre, approximate=False).astype(jnp.bfloat16)
    output = (
        middle.astype(jnp.float32)
        + jnp.dot(hidden_act, outer_w, preferred_element_type=jnp.float32)
    ).astype(jnp.bfloat16)
    return (normed, hidden_pre, hidden_act, output)


def channel_backward(middle, normed, hidden_pre, hidden_act, grad_out, inner_w, outer_w):
    grad_act = by_transpose(grad_out, outer_w)
    grad_outer = over_rows(hidden_act, grad_out)
    _, pullback = jax.vjp(lambda inputs: jax.nn.gelu(inputs, approximate=False), hidden_pre)
    grad_pre = pullback(grad_act)[0].astype(jnp.bfloat16)
    grad_norm = by_transpose(grad_pre, inner_w)
    grad_inner = over_rows(normed, grad_pre)
    grad_middle = (grad_out.astype(jnp.float32) + norm_back(middle, grad_norm)).astype(jnp.bfloat16)
    return (grad_middle, grad_inner, grad_outer)


def fold_rims(grad_ext):
    col_edges = jnp.concatenate([grad_ext[:, :HALF], grad_ext[:, -HALF:]], axis=1)
    col_recv = with_halo(col_edges.astype(jnp.bfloat16), (("cols", 1),), HALF, True).astype(
        col_edges.dtype
    )
    center = grad_ext[:, HALF:-HALF]
    center = jnp.concatenate(
        [
            center[:, :HALF] + col_recv[:, :HALF],
            center[:, HALF:-HALF],
            center[:, -HALF:] + col_recv[:, -HALF:],
        ],
        axis=1,
    )
    row_edges = jnp.concatenate([center[:HALF], center[-HALF:]], axis=0)
    row_recv = with_halo(row_edges.astype(jnp.bfloat16), (("rows", 0),), HALF, False).astype(
        row_edges.dtype
    )
    interior = center[HALF:-HALF]
    return jnp.concatenate(
        [
            interior[:HALF] + row_recv[:HALF],
            interior[HALF:-HALF],
            interior[-HALF:] + row_recv[-HALF:],
        ],
        axis=0,
    )


def reduce_grads(qkv_term, proj_term, inner_term, outer_term):
    row_count = lax.axis_size("rows")
    col_count = lax.axis_size("cols")
    tile_count = row_count * col_count
    reduced = (
        lax.psum_scatter(
            qkv_term.astype(jnp.bfloat16), "cols", scatter_dimension=1, tiled=True
        ).astype(jnp.float32),
        lax.psum_scatter(
            proj_term.astype(jnp.bfloat16), "cols", scatter_dimension=1, tiled=True
        ).astype(jnp.float32),
        lax.psum_scatter(
            inner_term.astype(jnp.bfloat16), "cols", scatter_dimension=1, tiled=True
        ).astype(jnp.float32),
        lax.psum_scatter(
            outer_term.astype(jnp.bfloat16), "cols", scatter_dimension=1, tiled=True
        ).astype(jnp.float32),
    )
    reduced = (
        lax.psum_scatter(
            reduced[0].astype(jnp.bfloat16), "rows", scatter_dimension=0, tiled=True
        ).astype(jnp.float32),
        lax.psum_scatter(
            reduced[1].astype(jnp.bfloat16), "rows", scatter_dimension=0, tiled=True
        ).astype(jnp.float32),
        lax.psum_scatter(
            reduced[2].astype(jnp.bfloat16), "rows", scatter_dimension=0, tiled=True
        ).astype(jnp.float32),
        lax.psum_scatter(
            reduced[3].astype(jnp.bfloat16), "rows", scatter_dimension=0, tiled=True
        ).astype(jnp.float32),
    )
    return tuple((section / tile_count for section in reduced))


def local(
    tokens,
    region_ids,
    upper_rim,
    upper_ids,
    lower_rim,
    lower_ids,
    cotangent,
    qkv_weight,
    proj_weight,
    inner_weight,
    outer_weight,
    bias_table,
):
    tile_rows, tile_cols, channels = tokens.shape
    row_index = lax.axis_index("rows")
    row_count = lax.axis_size("rows")
    tile_count = row_count * lax.axis_size("cols")
    normed_one, qkv_one, probs_one, mix_one = mixer_forward(
        tokens, region_ids, qkv_weight[0], bias_table[0]
    )
    mix_flat_one = mix_one.reshape(tile_rows * tile_cols, channels)
    middle_one = (
        tokens.reshape(-1, channels).astype(jnp.float32)
        + jnp.dot(mix_flat_one, proj_weight[0], preferred_element_type=jnp.float32)
    ).astype(jnp.bfloat16)
    chan_one = channel_forward(middle_one, inner_weight[0], outer_weight[0])
    first_out = chan_one[3].reshape(tile_rows, tile_cols, channels)
    region_low = region_ids.astype(jnp.bfloat16)
    row_ext, row_ids = (
        with_halo(first_out, (("rows", 0),), HALF, False),
        with_halo(region_low, (("rows", 0),), HALF, False),
    )
    at_top = row_index == 0
    at_bottom = row_index == row_count - 1
    row_ext = jnp.concatenate(
        [
            jnp.where(at_top, upper_rim, row_ext[:HALF]),
            row_ext[HALF:-HALF],
            jnp.where(at_bottom, lower_rim, row_ext[-HALF:]),
        ],
        axis=0,
    )
    row_ids = jnp.concatenate(
        [
            jnp.where(at_top, upper_ids.astype(jnp.bfloat16), row_ids[:HALF]),
            row_ids[HALF:-HALF],
            jnp.where(at_bottom, lower_ids.astype(jnp.bfloat16), row_ids[-HALF:]),
        ],
        axis=0,
    )
    extended, ext_ids = (
        with_halo(row_ext, (("cols", 1),), HALF, True),
        with_halo(row_ids, (("cols", 1),), HALF, True),
    )
    ext_region = ext_ids.astype(jnp.int32)
    normed_two, qkv_two, probs_two, mix_ext = mixer_forward(
        extended, ext_region, qkv_weight[1], bias_table[1]
    )
    mix_flat_two = mix_ext[HALF : HALF + tile_rows, HALF : HALF + tile_cols].reshape(
        tile_rows * tile_cols, channels
    )
    middle_two = (
        chan_one[3].astype(jnp.float32)
        + jnp.dot(mix_flat_two, proj_weight[1], preferred_element_type=jnp.float32)
    ).astype(jnp.bfloat16)
    chan_two = channel_forward(middle_two, inner_weight[1], outer_weight[1])
    grad_out = cotangent.reshape(-1, channels)
    grad_mid_two, inner_two, outer_two = channel_backward(
        middle_two,
        chan_two[0],
        chan_two[1],
        chan_two[2],
        grad_out,
        inner_weight[1],
        outer_weight[1],
    )
    proj_two = over_rows(mix_flat_two, grad_mid_two)
    grad_mix_two = (
        by_transpose(grad_mid_two, proj_weight[1])
        .astype(jnp.bfloat16)
        .reshape(tile_rows, tile_cols, channels)
    )
    grad_mix_ext = jnp.pad(grad_mix_two, ((HALF, HALF), (HALF, HALF), (0, 0)))
    grad_ext, qkv_two_grad, table_two = mixer_backward(
        extended, normed_two, qkv_two, probs_two, grad_mix_ext, qkv_weight[1]
    )
    folded = fold_rims(grad_ext)
    grad_first = (
        grad_mid_two.reshape(tile_rows, tile_cols, channels).astype(jnp.float32) + folded
    ).astype(jnp.bfloat16)
    summed_two = reduce_grads(qkv_two_grad, proj_two, inner_two, outer_two)
    grad_mid_one, inner_one, outer_one = channel_backward(
        middle_one,
        chan_one[0],
        chan_one[1],
        chan_one[2],
        grad_first.reshape(-1, channels),
        inner_weight[0],
        outer_weight[0],
    )
    proj_one = over_rows(mix_flat_one, grad_mid_one)
    grad_mix_one = (
        by_transpose(grad_mid_one, proj_weight[0])
        .astype(jnp.bfloat16)
        .reshape(tile_rows, tile_cols, channels)
    )
    grad_tokens, qkv_one_grad, table_one = mixer_backward(
        tokens, normed_one, qkv_one, probs_one, grad_mix_one, qkv_weight[0]
    )
    token_grad = (
        grad_mid_one.reshape(tile_rows, tile_cols, channels).astype(jnp.float32) + grad_tokens
    ).astype(jnp.bfloat16)
    summed_one = reduce_grads(qkv_one_grad, proj_one, inner_one, outer_one)
    table_sum = lax.psum(jnp.stack([table_one, table_two]), ("rows", "cols"))
    qkv_grad = jnp.stack([summed_one[0], summed_two[0]])
    proj_grad = jnp.stack([summed_one[1], summed_two[1]])
    inner_grad = jnp.stack([summed_one[2], summed_two[2]])
    outer_grad = jnp.stack([summed_one[3], summed_two[3]])
    return (token_grad, qkv_grad, proj_grad, inner_grad, outer_grad, table_sum / tile_count)


def solution(mesh):
    return jax.shard_map(
        local,
        mesh=mesh,
        in_specs=(
            P("rows", "cols", None),
            P("rows", "cols"),
            P(None, "cols", None),
            P(None, "cols"),
            P(None, "cols", None),
            P(None, "cols"),
            P("rows", "cols", None),
            P(),
            P(),
            P(),
            P(),
            P(),
        ),
        out_specs=(
            P("rows", "cols", None),
            P(None, "rows", "cols"),
            P(None, "rows", "cols"),
            P(None, "rows", "cols"),
            P(None, "rows", "cols"),
            P(),
        ),
        check_vma=False,
    )
```

profile of v0, /device:TPU:16, one launch (start us, length us, event | category | flops | bytes accessed | tf_op | source)
XLA Modules:
  0.0 740.8 jit_solution(4633801604680968060)
XLA Ops:
  8.5 4.8 collective-permute-start.4
  33.3 5.2 collective-permute-start
  44.7 6.0 collective-permute-start.7
  52.6 4.1 collective-permute-start.2
  56.7 3.9 collective-permute-start.3
  94.4 4.0 copy.147
  98.4 5.6 convert_element_type.304
  118.7 4.7 collective-permute-start.9
  125.2 4.7 collective-permute-start.10
  132.0 6.0 collective-permute-done.11
  146.3 68.5 %fusion.122 = (bf16[192,24]{0,1:T(8,128)(2,1)S(1)}, bf16[192,24]{0,1:T(8,128)(2,1)S(1)}, bf16[192,8]{0,1:T(8,128)(2,1)S(1)}, bf16[192,8]{0,1:T(8,128)(2,1)S(1)},...) fusion(bf16[192,576]{0,1:T(8,128)(2,1)} %convolution_convert_fusion.9, ...), kind=kCustom, calls=%all-reduce-scatter.6 | all-reduce-scatter fusion | flops 786434 | bytes 1230848
  214.8 20.4 %collective-permute-start.51 = (bf16[768,6]{0,1:T(8,128)(2,1)S(1)}, bf16[768,6]{0,1:T(8,128)(2,1)S(1)}, u32[]{:S(2)}, u32[]{:S(2)}) collective-permute-start(bf16[768,6]{0,1:T(8,128)(2,1)S(1)} %slice.212), channel_id=1, source_target_pairs={{0,8},{1,9},{2,10},{3,11},{4,12},{5,13},{6,14},{7,15},{8,16},{9,17... | collective-permute-start | bytes 27656
  243.0 4.6 collective-permute-start.46
  271.9 3.3 collective-permute-start.53
  304.3 4.6 collective-permute-start.38
  313.2 4.2 collective-permute-start.34
  321.4 104.6 %psum.7 = f32[2,225,6]{1,2,0:T(8,128)S(1)} all-reduce(f32[2,225,6]{1,2,0:T(8,128)S(1)} %pad_maximum_fusion.16), channel_id=1, replica_groups=mesh['rows'=16,'cols'=32] {'rows','cols'}, use_global_device_ids=true, to_apply=%region_40.41 | all-reduce | flops 2700 | bytes 21600 | tf_op jit(solution)/shard_map/psum | solution.py:379
  431.1 4.8 collective-permute-start.29
  437.9 4.4 collective-permute-start.27
  443.7 5.6 collective-permute-start.26
  449.3 3.9 collective-permute-start.25
  494.6 51.3 %reduce-scatter.29.cloned.1.call-done = bf16[192,24]{0,1:T(8,128)(2,1)} async-done(((bf16[192,768]{0,1:T(8,128)(2,1)}), bf16[192,24]{0,1:T(8,128)(2,1)}) %reduce-scatter.29.cloned.1.call-update) | async-done | bytes 9232 | tf_op jit(solution)/shard_map/reduce_scatter | solution.py:241
  545.9 121.3 %reduce-scatter.27.cloned.1.call-done = bf16[192,24]{0,1:T(8,128)(2,1)} async-done(((bf16[192,768]{0,1:T(8,128)(2,1)}), bf16[192,24]{0,1:T(8,128)(2,1)}) %reduce-scatter.27.cloned.1.call-update) | async-done | bytes 9232 | tf_op jit(solution)/shard_map/reduce_scatter | solution.py:241
  667.2 64.4 %all-reduce.19 = (bf16[192,18]{0,1:T(8,128)(2,1)S(1)}, bf16[192,18]{0,1:T(8,128)(2,1)S(1)}, bf16[192,6]{0,1:T(8,128)(2,1)S(1)}, bf16[192,6]{0,1:T(8,128)(2,1)S(1...) all-reduce(bf16[192,18]{0,1:T(8,128)(2,1)S(1)} %constant_dynamic-sl, ...), channel_id=5, replica_groups=mesh['rows'=16,'cols'=32] {'rows'}, use_global_device_ids=true, to_apply=%region_25.26.clone | all-reduce | flops 18432 | bytes 73728
  (456 shorter events, 207.3 us)
Async XLA Ops:
  7.2 485.2 %reduce-scatter.31.cloned.1.call-start = ((), (), s32[]{:S(2)}) async-start(), calls=%async_computation.6 | async-start | bytes 208896
  8.5 33.5 %collective-permute-start.4 = (bf16[4,32]{1,0:T(4,128)(2,1)}, bf16[4,32]{1,0:T(4,128)(2,1)}, u32[]{:S(2)}, u32[]{:S(2)}) collective-permute-start(bf16[4,32]{1,0:T(4,128)(2,1)} %get-tuple-element.76), channel_id=1, source_target_pairs={{0,32},{32,64},{64,96},{96,128},{128,160},{160,192},{192,224},{224... | collective-permute-start | bytes 776 | tf_op jit(solution)/shard_map/ppermute | solution.py:20
  13.4 28.6 %collective-permute-start.5 = (bf16[4,32]{1,0:T(4,128)(2,1)}, bf16[4,32]{1,0:T(4,128)(2,1)}, u32[]{:S(2)}, u32[]{:S(2)}) collective-permute-start(bf16[4,32]{1,0:T(4,128)(2,1)} %get-tuple-element.77), channel_id=1, source_target_pairs={{32,0},{64,32},{96,64},{128,96},{160,128},{192,160},{224,192},{256... | collective-permute-start | bytes 776 | tf_op jit(solution)/shard_map/ppermute | solution.py:23
  31.9 20.6 %collective-permute-start.1 = (bf16[4,32,192]{2,1,0:T(8,128)(2,1)S(1)}, bf16[4,32,192]{2,1,0:T(8,128)(2,1)S(1)}, u32[]{:S(2)}, u32[]{:S(2)}) collective-permute-start(bf16[4,32,192]{2,1,0:T(8,128)(2,1)S(1)} %bitcast.340), channel_id=1, source_target_pairs={{32,0},{64,32},{96,64},{128,96},{160,128},{192,160},{224,192},{256... | collective-permute-start | bytes 147464 | tf_op jit(solution)/shard_map/ppermute | solution.py:23
  33.3 19.3 %collective-permute-start = (bf16[4,32,192]{2,1,0:T(8,128)(2,1)S(1)}, bf16[4,32,192]{2,1,0:T(8,128)(2,1)S(1)}, u32[]{:S(2)}, u32[]{:S(2)}) collective-permute-start(bf16[4,32,192]{2,1,0:T(8,128)(2,1)S(1)} %bitcast.341), channel_id=1, source_target_pairs={{0,32},{32,64},{64,96},{96,128},{128,160},{160,192},{192,224},{224... | collective-permute-start | bytes 147464 | tf_op jit(solution)/shard_map/ppermute | solution.py:20
  214.8 28.2 %collective-permute-start.51 = (bf16[768,6]{0,1:T(8,128)(2,1)S(1)}, bf16[768,6]{0,1:T(8,128)(2,1)S(1)}, u32[]{:S(2)}, u32[]{:S(2)}) collective-permute-start(bf16[768,6]{0,1:T(8,128)(2,1)S(1)} %slice.212), channel_id=1, source_target_pairs={{0,8},{1,9},{2,10},{3,11},{4,12},{5,13},{6,14},{7,15},{8,16},{9,17... | collective-permute-start | bytes 27656
  252.1 19.8 %collective-permute-start.58 = (bf16[768,8]{0,1:T(8,128)(2,1)S(1)}, bf16[768,8]{0,1:T(8,128)(2,1)S(1)}, u32[]{:S(2)}, u32[]{:S(2)}) collective-permute-start(bf16[768,8]{0,1:T(8,128)(2,1)S(1)} %get-tuple-element.40), channel_id=1, source_target_pairs={{0,7},{1,8},{2,9},{3,10},{4,11},{5,12},{6,13},{7,14},{8,15},{9,16}... | collective-permute-start | bytes 36872
  254.0 21.2 %collective-permute-start.57 = (bf16[768,8]{0,1:T(8,128)(2,1)S(1)}, bf16[768,8]{0,1:T(8,128)(2,1)S(1)}, u32[]{:S(2)}, u32[]{:S(2)}) collective-permute-start(bf16[768,8]{0,1:T(8,128)(2,1)S(1)} %get-tuple-element.40), channel_id=1, source_target_pairs={{0,6},{1,7},{2,8},{3,9},{4,10},{5,11},{6,12},{7,13},{8,14},{9,15},... | collective-permute-start | bytes 36872
  278.1 215.1 %reduce-scatter.33.cloned.1.call-start = ((), (), s32[]{:S(2)}) async-start(), calls=%async_computation.7 | async-start | bytes 208896
  284.5 261.4 %reduce-scatter.29.cloned.1.call-start = ((), (), s32[]{:S(2)}) async-start(), calls=%async_computation.5 | async-start | bytes 405504 | tf_op jit(solution)/shard_map/reduce_scatter | solution.py:241
  286.2 381.0 %reduce-scatter.27.cloned.1.call-start = ((), (), s32[]{:S(2)}) async-start(), calls=%async_computation.4 | async-start | bytes 405504 | tf_op jit(solution)/shard_map/reduce_scatter | solution.py:241
  287.5 21.5 %collective-permute-start.42 = (bf16[192,8]{0,1:T(8,128)(2,1)S(1)}, bf16[192,8]{0,1:T(8,128)(2,1)S(1)}, u32[]{:S(2)}, u32[]{:S(2)}) collective-permute-start(bf16[192,8]{0,1:T(8,128)(2,1)S(1)} %get-tuple-element.38), channel_id=1, source_target_pairs={{0,7},{1,8},{2,9},{3,10},{4,11},{5,12},{6,13},{7,14},{8,15},{9,16}... | collective-permute-start | bytes 9224
  289.5 21.6 %collective-permute-start.41 = (bf16[192,8]{0,1:T(8,128)(2,1)S(1)}, bf16[192,8]{0,1:T(8,128)(2,1)S(1)}, u32[]{:S(2)}, u32[]{:S(2)}) collective-permute-start(bf16[192,8]{0,1:T(8,128)(2,1)S(1)} %get-tuple-element.38), channel_id=1, source_target_pairs={{0,6},{1,7},{2,8},{3,9},{4,10},{5,11},{6,12},{7,13},{8,14},{9,15},... | collective-permute-start | bytes 9224
  291.4 21.8 %collective-permute-start.40 = (bf16[192,8]{0,1:T(8,128)(2,1)S(1)}, bf16[192,8]{0,1:T(8,128)(2,1)S(1)}, u32[]{:S(2)}, u32[]{:S(2)}) collective-permute-start(bf16[192,8]{0,1:T(8,128)(2,1)S(1)} %get-tuple-element.38), channel_id=1, source_target_pairs={{0,5},{1,6},{2,7},{3,8},{4,9},{5,10},{6,11},{7,12},{8,13},{9,14},{... | collective-permute-start | bytes 9224
  308.9 117.0 %collective-permute-start.37 = (bf16[192,8]{0,1:T(8,128)(2,1)S(1)}, bf16[192,8]{0,1:T(8,128)(2,1)S(1)}, u32[]{:S(2)}, u32[]{:S(2)}) collective-permute-start(bf16[192,8]{0,1:T(8,128)(2,1)S(1)} %get-tuple-element.38), channel_id=1, source_target_pairs={{0,2},{1,3},{2,4},{3,5},{4,6},{5,7},{6,8},{7,9},{8,10},{9,11},{10,... | collective-permute-start | bytes 9224
  311.1 118.1 %collective-permute-start.36 = (bf16[192,8]{0,1:T(8,128)(2,1)S(1)}, bf16[192,8]{0,1:T(8,128)(2,1)S(1)}, u32[]{:S(2)}, u32[]{:S(2)}) collective-permute-start(bf16[192,8]{0,1:T(8,128)(2,1)S(1)} %get-tuple-element.38), channel_id=1, source_target_pairs={{0,1},{1,2},{2,3},{3,4},{4,5},{5,6},{6,7},{7,8},{8,9},{9,10},{10,1... | collective-permute-start | bytes 9224
  313.2 117.9 %collective-permute-start.34 = (bf16[192,8]{0,1:T(8,128)(2,1)S(1)}, bf16[192,8]{0,1:T(8,128)(2,1)S(1)}, u32[]{:S(2)}, u32[]{:S(2)}) collective-permute-start(bf16[192,8]{0,1:T(8,128)(2,1)S(1)} %get-tuple-element.39), channel_id=1, source_target_pairs={{0,7},{1,8},{2,9},{3,10},{4,11},{5,12},{6,13},{7,14},{8,15},{9,16}... | collective-permute-start | bytes 9224
  317.5 118.5 %collective-permute-start.33 = (bf16[192,8]{0,1:T(8,128)(2,1)S(1)}, bf16[192,8]{0,1:T(8,128)(2,1)S(1)}, u32[]{:S(2)}, u32[]{:S(2)}) collective-permute-start(bf16[192,8]{0,1:T(8,128)(2,1)S(1)} %get-tuple-element.39), channel_id=1, source_target_pairs={{0,6},{1,7},{2,8},{3,9},{4,10},{5,11},{6,12},{7,13},{8,14},{9,15},... | collective-permute-start | bytes 9224
  319.4 118.5 %collective-permute-start.32 = (bf16[192,8]{0,1:T(8,128)(2,1)S(1)}, bf16[192,8]{0,1:T(8,128)(2,1)S(1)}, u32[]{:S(2)}, u32[]{:S(2)}) collective-permute-start(bf16[192,8]{0,1:T(8,128)(2,1)S(1)} %get-tuple-element.39), channel_id=1, source_target_pairs={{0,5},{1,6},{2,7},{3,8},{4,9},{5,10},{6,11},{7,12},{8,13},{9,14},{... | collective-permute-start | bytes 9224
  426.0 17.8 %collective-permute-start.31 = (bf16[192,8]{0,1:T(8,128)(2,1)S(1)}, bf16[192,8]{0,1:T(8,128)(2,1)S(1)}, u32[]{:S(2)}, u32[]{:S(2)}) collective-permute-start(bf16[192,8]{0,1:T(8,128)(2,1)S(1)} %get-tuple-element.39), channel_id=1, source_target_pairs={{0,4},{1,5},{2,6},{3,7},{4,8},{5,9},{6,10},{7,11},{8,12},{9,13},{1... | collective-permute-start | bytes 9224
  429.2 20.1 %collective-permute-start.30 = (bf16[192,8]{0,1:T(8,128)(2,1)S(1)}, bf16[192,8]{0,1:T(8,128)(2,1)S(1)}, u32[]{:S(2)}, u32[]{:S(2)}) collective-permute-start(bf16[192,8]{0,1:T(8,128)(2,1)S(1)} %get-tuple-element.39), channel_id=1, source_target_pairs={{0,3},{1,4},{2,5},{3,6},{4,7},{5,8},{6,9},{7,10},{8,11},{9,12},{10... | collective-permute-start | bytes 9224
  431.1 22.2 %collective-permute-start.29 = (bf16[192,8]{0,1:T(8,128)(2,1)S(1)}, bf16[192,8]{0,1:T(8,128)(2,1)S(1)}, u32[]{:S(2)}, u32[]{:S(2)}) collective-permute-start(bf16[192,8]{0,1:T(8,128)(2,1)S(1)} %get-tuple-element.39), channel_id=1, source_target_pairs={{0,2},{1,3},{2,4},{3,5},{4,6},{5,7},{6,8},{7,9},{8,10},{9,11},{10,... | collective-permute-start | bytes 9224
  435.9 19.3 %collective-permute-start.28 = (bf16[192,8]{0,1:T(8,128)(2,1)S(1)}, bf16[192,8]{0,1:T(8,128)(2,1)S(1)}, u32[]{:S(2)}, u32[]{:S(2)}) collective-permute-start(bf16[192,8]{0,1:T(8,128)(2,1)S(1)} %get-tuple-element.39), channel_id=1, source_target_pairs={{0,1},{1,2},{2,3},{3,4},{4,5},{5,6},{6,7},{7,8},{8,9},{9,10},{10,1... | collective-permute-start | bytes 9224
  437.9 19.3 %collective-permute-start.27 = (bf16[192,18]{0,1:T(8,128)(2,1)S(1)}, bf16[192,18]{0,1:T(8,128)(2,1)S(1)}, u32[]{:S(2)}, u32[]{:S(2)}) collective-permute-start(bf16[192,18]{0,1:T(8,128)(2,1)S(1)} %slice.209), channel_id=1, source_target_pairs={{0,8},{1,9},{2,10},{3,11},{4,12},{5,13},{6,14},{7,15},{8,16},{9,17... | collective-permute-start | bytes 20744
  (112 other events, 1357.6 us)
Sparse Core Ops, SparseCore 0:
  278.2 76.3 reduce-scatter.30
  357.3 69.7 reduce-scatter.32
  431.8 114.0 reduce-scatter.28
  550.3 116.8 reduce-scatter.26
where the time goes:
time: 751 us; the launch traced here: 741 us
  blocking collectives  237 us (32%)
  waiting for transfers between devices  193 us (26%)
  starting transfers between devices  182 us (24%)
  local copies, waits for them, and re-layouts  55.5 us (7%)
  matrix products  40.7 us (5%)
  between operations  18.5 us (2%)
  other arithmetic  14.1 us (2%)
    reduce_scatter x2, waiting for transfers between devices, reduce_grads(): lax.psum_scatter(inner_term.astype(jnp.bfloat16), 'cols', scatter_dimensi...  173 us
    unnamed x50, starting transfers between devices  139 us
    unnamed x2, blocking collectives  133 us
    psum x1, blocking collectives, local(): table_sum = lax.psum(jnp.stack([table_one, table_two]), ('rows', 'cols'))  105 us
    ppermute x6, starting transfers between devices, with_halo(): lax.ppermute(lax.slice_in_dim(block, block.shape[dim] - width, None, axis...  24 us
    unnamed x173, local copies, waits for them, and re-layouts  19 us
    ppermute x6, starting transfers between devices, with_halo(): lax.ppermute(lax.slice_in_dim(block, 0, width, axis=dim), axis, backward)  18.5 us
  transfers between devices with their start and end apart: 64, of which 13 were waited for; matrix products, arithmetic and copies ran while one was open for 6% of the time, Pallas kernels for 0%

commit v1 on v0

--- a/solution.py
+++ b/solution.py
@@ -376,7 +376,7 @@
         grad_mid_one.reshape(tile_rows, tile_cols, channels).astype(jnp.float32) + grad_tokens
     ).astype(jnp.bfloat16)
     summed_one = reduce_grads(qkv_one_grad, proj_one, inner_one, outer_one)
-    table_sum = lax.psum(jnp.stack([table_one, table_two]), ("rows", "cols"))
+    table_sum = jnp.sum(lax.all_gather(jnp.stack([table_one, table_two]), ("rows", "cols")), axis=0)
     qkv_grad = jnp.stack([summed_one[0], summed_two[0]])
     proj_grad = jnp.stack([summed_one[1], summed_two[1]])
     inner_grad = jnp.stack([summed_one[2], summed_two[2]])

time: 751 us -> 1140 us (1.52)
  the two profiles are of different devices: /device:TPU:16 before, /device:TPU:8 now
where the time goes in v1:
time: 1140 us; the launch traced here: 1130 us
  waiting for transfers between devices  677 us (59%)
  starting transfers between devices  176 us (15%)
  blocking collectives  139 us (12%)
  local copies, waits for them, and re-layouts  55.3 us (5%)
  matrix products  40.6 us (4%)
  between operations  20 us (2%)
  other arithmetic  18.3 us (2%)
    all_gather x1, waiting for transfers between devices, local(): lax.all_gather(jnp.stack([table_one, table_two]), ('rows', 'cols'))  384 us
    reduce_scatter x2, waiting for transfers between devices, reduce_grads(): lax.psum_scatter(inner_term.astype(jnp.bfloat16), 'cols', scatter_dimensi...  238 us
    unnamed x2, blocking collectives  139 us
    unnamed x50, starting transfers between devices  134 us
    unnamed x55, waiting for transfers between devices  46.3 us
    ppermute x6, starting transfers between devices, with_halo(): lax.ppermute(lax.slice_in_dim(block, block.shape[dim] - width, None, axis...  23.3 us
  transfers between devices with their start and end apart: 65, of which 13 were waited for; matrix products, arithmetic and copies ran while one was open for 4% of the time, Pallas kernels for 0%

profile of v1, /device:TPU:8, one launch (start us, length us, event | category | flops | bytes accessed | tf_op | source)
XLA Modules:
  0.0 1126.1 jit_solution(16075841971525365612)
XLA Ops:
  8.8 4.3 collective-permute-start.4
  32.6 5.5 collective-permute-start
  43.7 6.0 collective-permute-start.7
  51.6 4.1 collective-permute-start.2
  98.1 5.6 convert_element_type.304
  118.3 4.7 collective-permute-start.9
  124.8 4.3 collective-permute-start.10
  131.2 6.1 collective-permute-done.11
  145.6 74.5 %fusion.122 = (bf16[192,24]{0,1:T(8,128)(2,1)}, bf16[192,24]{0,1:T(8,128)(2,1)}, bf16[192,8]{0,1:T(8,128)(2,1)S(1)}, bf16[192,8]{0,1:T(8,128)(2,1)S(1)}, bf16[76...) fusion(bf16[192,576]{0,1:T(8,128)(2,1)} %convolution_convert_fusion.9, ...), kind=kCustom, calls=%all-reduce-scatter.6 | all-reduce-scatter fusion | flops 786434 | bytes 1230848
  220.0 5.7 collective-permute-start.51
  229.6 8.0 collective-permute-start.49
  237.6 4.6 collective-permute-start.48
  244.5 4.3 collective-permute-start.46
  301.5 4.9 collective-permute-start.39
  309.3 4.2 collective-permute-start.37
  315.5 4.9 collective-permute-start.34
  351.7 6.1 collective-permute-start.21
  359.7 5.9 collective-permute-start.18
  386.3 37.3 %reduce-scatter.33.cloned.1.call-done = bf16[48,6]{1,0:T(8,128)(2,1)} async-done(((bf16[768,6]{1,0:T(8,128)(2,1)}), bf16[48,6]{1,0:T(8,128)(2,1)}) %reduce-scatter.33.cloned.1.call-update) | async-done | bytes 592
  425.0 116.5 %reduce-scatter.29.cloned.1.call-done = bf16[192,24]{0,1:T(8,128)(2,1)} async-done(((bf16[192,768]{0,1:T(8,128)(2,1)}), bf16[192,24]{0,1:T(8,128)(2,1)}) %reduce-scatter.29.cloned.1.call-update) | async-done | bytes 9232 | tf_op jit(solution)/shard_map/reduce_scatter | solution.py:241
  541.5 121.4 %reduce-scatter.27.cloned.1.call-done = bf16[192,24]{0,1:T(8,128)(2,1)} async-done(((bf16[192,768]{0,1:T(8,128)(2,1)}), bf16[192,24]{0,1:T(8,128)(2,1)}) %reduce-scatter.27.cloned.1.call-update) | async-done | bytes 9232 | tf_op jit(solution)/shard_map/reduce_scatter | solution.py:241
  662.9 64.5 %all-reduce.19 = (bf16[192,18]{0,1:T(8,128)(2,1)S(1)}, bf16[192,18]{0,1:T(8,128)(2,1)S(1)}, bf16[192,6]{0,1:T(8,128)(2,1)S(1)}, bf16[192,6]{0,1:T(8,128)(2,1)S(1...) all-reduce(bf16[192,18]{0,1:T(8,128)(2,1)S(1)} %constant_dynamic-sl, ...), channel_id=6, replica_groups=mesh['rows'=16,'cols'=32] {'rows'}, use_global_device_ids=true, to_apply=%region_25.26.clone | all-reduce | flops 18432 | bytes 73728
  729.9 384.0 %all-gather.3.cloned.1.call-done = f32[1024,225,6]{1,2,0:T(8,128)} async-done(((f32[2,225,6]{1,2,0:T(8,128)}), f32[1024,225,6]{1,2,0:T(8,128)}) %all-gather.3.cloned.1.call-update) | async-done | bytes 5529616 | tf_op jit(solution)/shard_map/all_gather | solution.py:379
  1113.9 4.2 reduce_sum.245
  (471 shorter events, 214.4 us)
Async XLA Ops:
  8.0 377.5 %reduce-scatter.31.cloned.1.call-start = ((), (), s32[]{:S(2)}) async-start(), calls=%async_computation.7 | async-start | bytes 208896
  8.8 32.9 %collective-permute-start.4 = (bf16[4,32]{1,0:T(4,128)(2,1)S(1)}, bf16[4,32]{1,0:T(4,128)(2,1)S(1)}, u32[]{:S(2)}, u32[]{:S(2)}) collective-permute-start(bf16[4,32]{1,0:T(4,128)(2,1)S(1)} %get-tuple-element.76), channel_id=1, source_target_pairs={{0,32},{32,64},{64,96},{96,128},{128,160},{160,192},{192,224},{224... | collective-permute-start | bytes 776 | tf_op jit(solution)/shard_map/ppermute | solution.py:20
  13.1 28.6 %collective-permute-start.5 = (bf16[4,32]{1,0:T(4,128)(2,1)S(1)}, bf16[4,32]{1,0:T(4,128)(2,1)S(1)}, u32[]{:S(2)}, u32[]{:S(2)}) collective-permute-start(bf16[4,32]{1,0:T(4,128)(2,1)S(1)} %get-tuple-element.77), channel_id=1, source_target_pairs={{32,0},{64,32},{96,64},{128,96},{160,128},{192,160},{224,192},{256... | collective-permute-start | bytes 776 | tf_op jit(solution)/shard_map/ppermute | solution.py:23
  31.2 20.3 %collective-permute-start.1 = (bf16[4,32,192]{2,1,0:T(8,128)(2,1)S(1)}, bf16[4,32,192]{2,1,0:T(8,128)(2,1)S(1)}, u32[]{:S(2)}, u32[]{:S(2)}) collective-permute-start(bf16[4,32,192]{2,1,0:T(8,128)(2,1)S(1)} %bitcast.342), channel_id=1, source_target_pairs={{32,0},{64,32},{96,64},{128,96},{160,128},{192,160},{224,192},{256... | collective-permute-start | bytes 147464 | tf_op jit(solution)/shard_map/ppermute | solution.py:23
  32.6 18.9 %collective-permute-start = (bf16[4,32,192]{2,1,0:T(8,128)(2,1)S(1)}, bf16[4,32,192]{2,1,0:T(8,128)(2,1)S(1)}, u32[]{:S(2)}, u32[]{:S(2)}) collective-permute-start(bf16[4,32,192]{2,1,0:T(8,128)(2,1)S(1)} %bitcast.343), channel_id=1, source_target_pairs={{0,32},{32,64},{64,96},{96,128},{128,160},{160,192},{192,224},{224... | collective-permute-start | bytes 147464 | tf_op jit(solution)/shard_map/ppermute | solution.py:20
  220.0 24.4 %collective-permute-start.51 = (bf16[768,6]{0,1:T(8,128)(2,1)S(1)}, bf16[768,6]{0,1:T(8,128)(2,1)S(1)}, u32[]{:S(2)}, u32[]{:S(2)}) collective-permute-start(bf16[768,6]{0,1:T(8,128)(2,1)S(1)} %slice.212), channel_id=1, source_target_pairs={{0,8},{1,9},{2,10},{3,11},{4,12},{5,13},{6,14},{7,15},{8,16},{9,17... | collective-permute-start | bytes 27656
  225.7 23.1 %collective-permute-start.50 = (bf16[768,8]{0,1:T(8,128)(2,1)S(1)}, bf16[768,8]{0,1:T(8,128)(2,1)S(1)}, u32[]{:S(2)}, u32[]{:S(2)}) collective-permute-start(bf16[768,8]{0,1:T(8,128)(2,1)S(1)} %get-tuple-element.41), channel_id=1, source_target_pairs={{0,7},{1,8},{2,9},{3,10},{4,11},{5,12},{6,13},{7,14},{8,15},{9,16}... | collective-permute-start | bytes 36872
  229.6 21.7 %collective-permute-start.49 = (bf16[768,8]{0,1:T(8,128)(2,1)S(1)}, bf16[768,8]{0,1:T(8,128)(2,1)S(1)}, u32[]{:S(2)}, u32[]{:S(2)}) collective-permute-start(bf16[768,8]{0,1:T(8,128)(2,1)S(1)} %get-tuple-element.41), channel_id=1, source_target_pairs={{0,6},{1,7},{2,8},{3,9},{4,10},{5,11},{6,12},{7,13},{8,14},{9,15},... | collective-permute-start | bytes 36872
  237.6 15.6 %collective-permute-start.48 = (bf16[768,8]{0,1:T(8,128)(2,1)S(1)}, bf16[768,8]{0,1:T(8,128)(2,1)S(1)}, u32[]{:S(2)}, u32[]{:S(2)}) collective-permute-start(bf16[768,8]{0,1:T(8,128)(2,1)S(1)} %get-tuple-element.41), channel_id=1, source_target_pairs={{0,5},{1,6},{2,7},{3,8},{4,9},{5,10},{6,11},{7,12},{8,13},{9,14},{... | collective-permute-start | bytes 36872
  253.2 16.5 %collective-permute-start.58 = (bf16[768,8]{0,1:T(8,128)(2,1)S(1)}, bf16[768,8]{0,1:T(8,128)(2,1)S(1)}, u32[]{:S(2)}, u32[]{:S(2)}) collective-permute-start(bf16[768,8]{0,1:T(8,128)(2,1)S(1)} %get-tuple-element.40), channel_id=1, source_target_pairs={{0,7},{1,8},{2,9},{3,10},{4,11},{5,12},{6,13},{7,14},{8,15},{9,16}... | collective-permute-start | bytes 36872
  254.9 18.0 %collective-permute-start.57 = (bf16[768,8]{0,1:T(8,128)(2,1)S(1)}, bf16[768,8]{0,1:T(8,128)(2,1)S(1)}, u32[]{:S(2)}, u32[]{:S(2)}) collective-permute-start(bf16[768,8]{0,1:T(8,128)(2,1)S(1)} %get-tuple-element.40), channel_id=1, source_target_pairs={{0,6},{1,7},{2,8},{3,9},{4,10},{5,11},{6,12},{7,13},{8,14},{9,15},... | collective-permute-start | bytes 36872
  275.8 147.8 %reduce-scatter.33.cloned.1.call-start = ((), (), s32[]{:S(2)}) async-start(), calls=%async_computation.8 | async-start | bytes 208896
  282.1 259.4 %reduce-scatter.29.cloned.1.call-start = ((), (), s32[]{:S(2)}) async-start(), calls=%async_computation.5 | async-start | bytes 405504 | tf_op jit(solution)/shard_map/reduce_scatter | solution.py:241
  283.3 379.6 %reduce-scatter.27.cloned.1.call-start = ((), (), s32[]{:S(2)}) async-start(), calls=%async_computation.4 | async-start | bytes 405504 | tf_op jit(solution)/shard_map/reduce_scatter | solution.py:241
  284.9 829.0 %all-gather.3.cloned.1.call-start = ((), (), s32[]{:S(2)}) async-start(), calls=%async_computation.6 | async-start | bytes 8404992 | tf_op jit(solution)/shard_map/all_gather | solution.py:379
  291.2 18.1 %collective-permute-start.42 = (bf16[192,8]{0,1:T(8,128)(2,1)S(1)}, bf16[192,8]{0,1:T(8,128)(2,1)S(1)}, u32[]{:S(2)}, u32[]{:S(2)}) collective-permute-start(bf16[192,8]{0,1:T(8,128)(2,1)S(1)} %get-tuple-element.38), channel_id=1, source_target_pairs={{0,7},{1,8},{2,9},{3,10},{4,11},{5,12},{6,13},{7,14},{8,15},{9,16}... | collective-permute-start | bytes 9224
  292.6 20.9 %collective-permute-start.41 = (bf16[192,8]{0,1:T(8,128)(2,1)S(1)}, bf16[192,8]{0,1:T(8,128)(2,1)S(1)}, u32[]{:S(2)}, u32[]{:S(2)}) collective-permute-start(bf16[192,8]{0,1:T(8,128)(2,1)S(1)} %get-tuple-element.38), channel_id=1, source_target_pairs={{0,6},{1,7},{2,8},{3,9},{4,10},{5,11},{6,12},{7,13},{8,14},{9,15},... | collective-permute-start | bytes 9224
  294.2 21.3 %collective-permute-start.40 = (bf16[192,8]{0,1:T(8,128)(2,1)S(1)}, bf16[192,8]{0,1:T(8,128)(2,1)S(1)}, u32[]{:S(2)}, u32[]{:S(2)}) collective-permute-start(bf16[192,8]{0,1:T(8,128)(2,1)S(1)} %get-tuple-element.38), channel_id=1, source_target_pairs={{0,5},{1,6},{2,7},{3,8},{4,9},{5,10},{6,11},{7,12},{8,13},{9,14},{... | collective-permute-start | bytes 9224
  301.5 18.9 %collective-permute-start.39 = (bf16[192,8]{0,1:T(8,128)(2,1)S(1)}, bf16[192,8]{0,1:T(8,128)(2,1)S(1)}, u32[]{:S(2)}, u32[]{:S(2)}) collective-permute-start(bf16[192,8]{0,1:T(8,128)(2,1)S(1)} %get-tuple-element.38), channel_id=1, source_target_pairs={{0,4},{1,5},{2,6},{3,7},{4,8},{5,9},{6,10},{7,11},{8,12},{9,13},{1... | collective-permute-start | bytes 9224
  339.0 18.8 %collective-permute-start.25 = (bf16[192,24]{0,1:T(8,128)(2,1)S(1)}, bf16[192,24]{0,1:T(8,128)(2,1)S(1)}, u32[]{:S(2)}, u32[]{:S(2)}) collective-permute-start(bf16[192,24]{0,1:T(8,128)(2,1)S(1)} %copy-done.53), channel_id=1, source_target_pairs={{0,6},{1,7},{2,8},{3,9},{4,10},{5,11},{6,12},{7,13},{8,14},{9,15},... | collective-permute-start | bytes 27656
  341.2 18.5 %collective-permute-start.24 = (bf16[192,24]{0,1:T(8,128)(2,1)S(1)}, bf16[192,24]{0,1:T(8,128)(2,1)S(1)}, u32[]{:S(2)}, u32[]{:S(2)}) collective-permute-start(bf16[192,24]{0,1:T(8,128)(2,1)S(1)} %copy-done.53), channel_id=1, source_target_pairs={{0,5},{1,6},{2,7},{3,8},{4,9},{5,10},{6,11},{7,12},{8,13},{9,14},{... | collective-permute-start | bytes 27656
  343.4 22.2 %collective-permute-start.23 = (bf16[192,24]{0,1:T(8,128)(2,1)S(1)}, bf16[192,24]{0,1:T(8,128)(2,1)S(1)}, u32[]{:S(2)}, u32[]{:S(2)}) collective-permute-start(bf16[192,24]{0,1:T(8,128)(2,1)S(1)} %copy-done.53), channel_id=1, source_target_pairs={{0,4},{1,5},{2,6},{3,7},{4,8},{5,9},{6,10},{7,11},{8,12},{9,13},{1... | collective-permute-start | bytes 27656
  348.3 19.5 %collective-permute-start.22 = (bf16[192,24]{0,1:T(8,128)(2,1)S(1)}, bf16[192,24]{0,1:T(8,128)(2,1)S(1)}, u32[]{:S(2)}, u32[]{:S(2)}) collective-permute-start(bf16[192,24]{0,1:T(8,128)(2,1)S(1)} %copy-done.53), channel_id=1, source_target_pairs={{0,3},{1,4},{2,5},{3,6},{4,7},{5,8},{6,9},{7,10},{8,11},{9,12},{10... | collective-permute-start | bytes 27656
  351.7 17.3 %collective-permute-start.21 = (bf16[192,24]{0,1:T(8,128)(2,1)S(1)}, bf16[192,24]{0,1:T(8,128)(2,1)S(1)}, u32[]{:S(2)}, u32[]{:S(2)}) collective-permute-start(bf16[192,24]{0,1:T(8,128)(2,1)S(1)} %copy-done.53), channel_id=1, source_target_pairs={{0,2},{1,3},{2,4},{3,5},{4,6},{5,7},{6,8},{7,9},{8,10},{9,11},{10,... | collective-permute-start | bytes 27656
  (119 other events, 1470.4 us)
Sparse Core Ops, SparseCore 0:
  275.9 74.5 reduce-scatter.30
  353.3 70.2 reduce-scatter.32
  428.2 113.2 reduce-scatter.28
  545.9 116.9 reduce-scatter.26
Sparse Core Ops, SparseCore 1:
  288.7 825.2 all-gather.2
